TPU v7x, 256 devices: a whole 4x4x8 slice. The times are simulated.
256 devices in a mesh: gx: 8 (over z), gy: 8 (over y, core), gz: 4 (over x).
Axes of the slice: x: 4, y: 4, z: 8, core: 2. Of those that a mesh axis runs over, the one named last changes fastest.
Arguments:
- x_block: float32 [16, 64, 32, 512], P(None, 'gx', 'gy', 'gz'), may hold values from -6 to 6
- p_block: float32 [16, 64, 32, 512], P(None, 'gx', 'gy', 'gz'), may hold values from -6 to 6
- voxel_class: int32 [64, 32, 512], P('gx', 'gy', 'gz'), may hold values from 0 to 7
- conductance: float32 [8], replicated, may hold values from 0.25 to 4
Outputs:
- x_next: float32 [16, 64, 32, 512], P(None, 'gx', 'gy', 'gz')
- p_next: float32 [16, 64, 32, 512], P(None, 'gx', 'gy', 'gz')
All inputs are finite; a program needn't handle non-finite values.
Results may differ from a plain program's by a relative error of at most 0.0003.
Values sent between devices are 32-bit elements; how exact they have to be, the bound alone decides.
No kernel may reach another device: no remote copies, remote signals or barrier semaphores. Data moves between devices by JAX's collectives and lax.ppermute only.
A program may use at most 64 MiB of HBM per device.

v0:
```python
import jax
import jax.numpy as jnp
from jax import lax
from jax.sharding import PartitionSpec as P

VECS = 16
CLASSES = 8
ITERS = 2
INNER = 4


jacobi_weight = 2.0 / 3.0
mass_shift = 0.05


def with_halo(array, sides, width):
    for axis, dim in sides:
        peers, length = (lax.axis_size(axis), array.shape[dim])
        up = [(i, (i + 1) % peers) for i in range(peers - 1)]
        down = [(j, i) for i, j in up]
        last = lax.slice_in_dim(array, length - width, length, axis=dim)
        leading = lax.slice_in_dim(array, 0, width, axis=dim)
        before = lax.ppermute(last, axis, up)
        after = lax.ppermute(leading, axis, down)
        array = jnp.concatenate([before, array, after], axis=dim)
    return array


def matmul_high(first_side, second_side):
    return jnp.dot(first_side, second_side, precision=lax.Precision.HIGHEST)


def harmonic(one_side, other_side):
    return 2.0 * one_side * other_side / (one_side + other_side)


def fine_edges(padded):
    edge_x = harmonic(padded[:-1, 1:-1, 1:-1], padded[1:, 1:-1, 1:-1])
    edge_y = harmonic(padded[1:-1, :-1, 1:-1], padded[1:-1, 1:, 1:-1])
    edge_z = harmonic(padded[1:-1, 1:-1, :-1], padded[1:-1, 1:-1, 1:])
    return (edge_x, edge_y, edge_z)


def pair_sum(values, axis_index):
    old_shape = values.shape
    new_shape = (
        old_shape[:axis_index] + (old_shape[axis_index] // 2, 2) + old_shape[axis_index + 1 :]
    )
    return jnp.sum(values.reshape(new_shape), axis=axis_index + 1)


def coarsen_edges(edges):
    edge_x, edge_y, edge_z = edges
    coarse_x = pair_sum(pair_sum(edge_x[0::2], 1), 2)
    coarse_y = pair_sum(pair_sum(edge_y[:, 0::2], 0), 2)
    coarse_z = pair_sum(pair_sum(edge_z[:, :, 0::2], 0), 1)
    return (coarse_x, coarse_y, coarse_z)


def diagonal_of(edges, shift_term):
    edge_x, edge_y, edge_z = edges
    return (
        shift_term
        + edge_x[:-1]
        + edge_x[1:]
        + edge_y[:, :-1]
        + edge_y[:, 1:]
        + edge_z[:, :, :-1]
        + edge_z[:, :, 1:]
    )


def apply_operator(padded, field, edges, diagonal):
    edge_x, edge_y, edge_z = edges
    beside = edge_x[1:] * padded[:, 2:, 1:-1, 1:-1] + edge_x[:-1] * padded[:, :-2, 1:-1, 1:-1]
    beside = (
        beside
        + edge_y[:, 1:] * padded[:, 1:-1, 2:, 1:-1]
        + edge_y[:, :-1] * padded[:, 1:-1, :-2, 1:-1]
    )
    beside = (
        beside
        + edge_z[:, :, 1:] * padded[:, 1:-1, 1:-1, 2:]
        + edge_z[:, :, :-1] * padded[:, 1:-1, 1:-1, :-2]
    )
    return diagonal * field - beside


def smooth(residual, level_data, rim_fn):
    edges, diagonal = level_data
    first = jacobi_weight * residual / diagonal
    return (
        first
        + jacobi_weight
        * (residual - apply_operator(rim_fn(first), first, edges, diagonal))
        / diagonal
    )


def restrict(field):
    return pair_sum(pair_sum(pair_sum(field, 1), 2), 3)


def prolong(field):
    channels, size_x, size_y, size_z = field.shape
    wide = jnp.broadcast_to(
        field[:, :, None, :, None, :, None], (channels, size_x, 2, size_y, 2, size_z, 2)
    )
    return wide.reshape(channels, 2 * size_x, 2 * size_y, 2 * size_z)


def precondition(residual, levels, rims):
    middle_res = restrict(residual)
    coarse_res = restrict(middle_res)
    fine_part = smooth(residual, levels[0], rims[0])
    middle_part = smooth(middle_res, levels[1], rims[1])
    coarse_part = smooth(coarse_res, levels[2], rims[2])
    return fine_part + prolong(middle_part + prolong(coarse_part))


def solve_small(gram, cross):
    factor = jnp.linalg.cholesky(gram)
    partial_solve = jax.scipy.linalg.solve_triangular(factor, cross, lower=True)
    return jax.scipy.linalg.solve_triangular(factor, partial_solve, lower=True, trans="T")


def ritz_step(gram_b, gram_a, num_vecs, inner_steps):
    inverse_root = 1.0 / jnp.sqrt(jnp.diagonal(gram_b))
    outer_scale = inverse_root[:, None] * inverse_root[None, :]
    sym_a = 0.5 * (gram_a + gram_a.T)
    normed_b = 0.5 * (gram_b + gram_b.T) * outer_scale
    normed_a = sym_a * outer_scale
    factor_b = jnp.linalg.cholesky(normed_b)
    factor_a = jnp.linalg.cholesky(normed_a)
    sub_basis = jnp.eye(normed_b.shape[0], num_vecs, dtype=jnp.float32)
    for inner_step in range(inner_steps):
        lifted = matmul_high(factor_b, sub_basis)
        solved = jax.scipy.linalg.solve_triangular(factor_a, lifted, lower=True)
        solved = jax.scipy.linalg.solve_triangular(factor_a, solved, lower=True, trans="T")
        mapped = matmul_high(factor_b.T, solved)
        small_factor = jnp.linalg.cholesky(matmul_high(mapped.T, mapped))
        sub_basis = jax.scipy.linalg.solve_triangular(small_factor, mapped.T, lower=True).T
    coefficients = inverse_root[:, None] * jax.scipy.linalg.solve_triangular(
        factor_b, sub_basis, lower=True, trans="T"
    )
    rayleigh = matmul_high(coefficients.T, matmul_high(sym_a, coefficients))
    return (coefficients, rayleigh)


def fine_rim(field):
    return with_halo(field, (("gx", 1), ("gy", 2), ("gz", 3)), 1)


def middle_rim(field):
    return with_halo(field, (("gx", 1), ("gy", 2), ("gz", 3)), 1)


def coarse_rim(field):
    return with_halo(field, (("gx", 1), ("gy", 2), ("gz", 3)), 1)


def on_device(x_block, p_block, voxel_class, conductance):
    device_cells = x_block.shape[1] * x_block.shape[2] * x_block.shape[3]
    all_cells = device_cells * lax.axis_size("gx") * lax.axis_size("gy") * lax.axis_size("gz")
    local_cond = jnp.zeros(voxel_class.shape, jnp.float32)
    for class_index in range(CLASSES):
        local_cond = local_cond + jnp.where(
            voxel_class == class_index, conductance[class_index], 0.0
        )
    padded_first = fine_rim(jnp.concatenate([local_cond[None], x_block], 0))
    cond_pad = padded_first[0]
    x_pad = padded_first[1:]
    p_pad = fine_rim(p_block)
    fine_edge = fine_edges(cond_pad)
    middle_edge = coarsen_edges(fine_edge)
    coarse_edge = coarsen_edges(middle_edge)
    levels = (
        (fine_edge, diagonal_of(fine_edge, mass_shift)),
        (middle_edge, diagonal_of(middle_edge, 8.0 * mass_shift)),
        (coarse_edge, diagonal_of(coarse_edge, 64.0 * mass_shift)),
    )
    rims = (fine_rim, middle_rim, coarse_rim)
    block_x, block_p = (x_block, p_block)
    applied_x = apply_operator(x_pad, block_x, levels[0][0], levels[0][1])
    applied_p = apply_operator(p_pad, block_p, levels[0][0], levels[0][1])
    for iteration in range(ITERS):
        flat_x = block_x.reshape(VECS, -1)
        flat_ax = applied_x.reshape(VECS, -1)
        gram_x, cross_x = lax.psum(
            (matmul_high(flat_x, flat_x.T), matmul_high(flat_x, flat_ax.T)), ("gx", "gy", "gz")
        )
        projected = solve_small(gram_x / all_cells, cross_x / all_cells)
        residual = applied_x - matmul_high(projected.T, flat_x).reshape(block_x.shape)
        block_w = precondition(residual, levels, rims)
        applied_w = apply_operator(fine_rim(block_w), block_w, levels[0][0], levels[0][1])
        search = jnp.concatenate([block_x, block_w, block_p], 0).reshape(3 * VECS, -1)
        applied = jnp.concatenate([applied_x, applied_w, applied_p], 0).reshape(3 * VECS, -1)
        gram_b, gram_a = lax.psum(
            (matmul_high(search, search.T), matmul_high(search, applied.T)), ("gx", "gy", "gz")
        )
        coefficients, rayleigh = ritz_step(gram_b / all_cells, gram_a / all_cells, VECS, INNER)
        tail = coefficients[VECS:]
        block_x = matmul_high(coefficients.T, search).reshape(x_block.shape)
        applied_x = matmul_high(coefficients.T, applied).reshape(x_block.shape)
        block_p = matmul_high(tail.T, search[VECS:]).reshape(x_block.shape)
        applied_p = matmul_high(tail.T, applied[VECS:]).reshape(x_block.shape)
    return (block_x, block_p)


def solution(mesh):
    in_specs = (P(None, "gx", "gy", "gz"), P(None, "gx", "gy", "gz"), P("gx", "gy", "gz"), P())
    out_specs = (P(None, "gx", "gy", "gz"), P(None, "gx", "gy", "gz"))
    return jax.shard_map(
        on_device, mesh=mesh, in_specs=in_specs, out_specs=out_specs, check_vma=False
    )
```

profile of v0, /device:TPU:8, one launch (start us, length us, event | category | flops | bytes accessed | tf_op | source)
XLA Modules:
  0.0 727.4 jit_solution(8951026829940790295)
XLA Ops:
  3.4 5.8 select_add_fusion
  10.5 4.5 collective-permute-start
  16.2 3.8 collective-permute-start.31
  28.4 2.4 collective-permute-start.33
  30.8 3.2 collective-permute-start.3
  34.0 1.9 collective-permute-start.2
  36.4 3.8 collective-permute-done.2
  41.0 3.4 collective-permute-start.4
  47.3 5.3 collective-permute-start.35
  57.2 79.8 %all-reduce.3 = (f32[16,16]{0,1:T(8,128)S(1)}, f32[16,16]{0,1:T(8,128)S(1)}) all-reduce(f32[16,16]{0,1:T(8,128)S(1)} %convolution_bitcast_fusion.8, f32[16,16]{0,1:T(8,128)S(1)} %convolution_bitcast_fusion.7), channel_id=1, replica_groups=mesh['gx'=8,'gy'=8,'gz'=4] {'gx','gy','gz'}, use_global_device_ids=true, to_apply=%region_0.1 | all-reduce | flops 512 | bytes 4096 | tf_op jit(solution)/shard_map/psum | solution.py:189
  146.5 4.5 collective-permute-start.13
  153.8 4.5 collective-permute-start.19
  158.4 2.1 fusion.56
  162.3 4.5 collective-permute-start.7
  166.9 1.9 collective-permute-start.20
  168.8 2.4 collective-permute-start.21
  171.4 3.0 collective-permute-done.21
  174.4 2.4 collective-permute-start.23
  178.2 1.9 collective-permute-start.14
  180.1 2.4 collective-permute-start.15
  183.3 2.2 collective-permute-done.15
  187.6 5.2 collective-permute-start.17
  195.6 13.0 %collective-permute-start.9 = (f32[16,10,1,128]{3,0,2,1:T(8,128)}, f32[16,10,1,128]{3,0,2,1:T(8,128)}, u32[]{:S(2)}, u32[]{:S(2)}) collective-permute-start(f32[16,10,1,128]{3,0,2,1:T(8,128)} %get-tuple-element.57), channel_id=1, source_target_pairs={{0,4},{4,8},{8,12},{12,16},{16,20},{20,24},{24,28},{1,5},{5,9},{9,... | collective-permute-start | bytes 245768 | tf_op jit(solution)/shard_map/ppermute | solution.py:23
  212.0 4.7 collective-permute-start.11
  221.6 6.0 collective-permute-done.11
  227.7 4.9 collective-permute-done.10
  235.4 4.5 collective-permute-start.25
  243.5 2.4 collective-permute-start.27
  246.0 3.3 collective-permute-done.27
  250.4 2.4 collective-permute-start.29
  259.6 2.4 collective-permute-done.29
  262.0 4.9 collective-permute-done.28
  269.2 76.2 %all-reduce.2 = (f32[48,48]{0,1:T(8,128)S(1)}, f32[48,48]{1,0:T(8,128)S(1)}) all-reduce(f32[48,48]{0,1:T(8,128)S(1)} %copy-done.55, f32[48,48]{1,0:T(8,128)S(1)} %convolution_bitcast_fusion.2), channel_id=1, replica_groups=mesh['gx'=8,'gy'=8,'gz'=4] {'gx','gy','gz'}, use_global_device_ids=true, to_apply=%region_24.28 | all-reduce | flops 4608 | bytes 36864 | tf_op jit(solution)/shard_map/psum | solution.py:198
  346.9 4.4 cholesky.247
  353.6 4.4 cholesky.258
  359.4 3.7 custom-call.60
  388.0 3.7 custom-call.62
  394.4 76.1 %all-reduce.1 = (f32[16,16]{0,1:T(8,128)S(1)}, f32[16,16]{0,1:T(8,128)S(1)}) all-reduce(f32[16,16]{0,1:T(8,128)S(1)} %fusion.318, f32[16,16]{0,1:T(8,128)S(1)} %fusion.319), channel_id=1, replica_groups=mesh['gx'=8,'gy'=8,'gz'=4] {'gx','gy','gz'}, use_global_device_ids=true, to_apply=%region_28.36 | all-reduce | flops 512 | bytes 4096 | tf_op jit(solution)/shard_map/psum | solution.py:189
  482.6 5.2 collective-permute-start.43
  489.7 4.5 collective-permute-start.49
  500.1 4.5 collective-permute-start.37
  504.7 1.9 collective-permute-start.50
  506.6 2.4 collective-permute-start.51
  512.4 2.3 collective-permute-start.53
  517.9 2.4 collective-permute-start.45
  521.8 3.1 collective-permute-start.38
  525.0 1.9 collective-permute-start.39
  528.4 5.2 collective-permute-start.47
  533.7 3.1 collective-permute-done.46
  541.4 5.2 collective-permute-start.41
  551.6 5.2 collective-permute-done.41
  556.8 4.9 collective-permute-done.40
  565.0 4.5 collective-permute-start.55
  571.2 2.2 collective-permute-start.56
  573.4 2.4 collective-permute-start.57
  575.9 3.3 collective-permute-done.57
  580.3 4.1 collective-permute-start.59
  588.0 5.2 collective-permute-done.59
  593.2 4.9 collective-permute-done.58
  601.3 76.8 %all-reduce = (f32[48,48]{1,0:T(8,128)S(1)}, f32[48,48]{1,0:T(8,128)S(1)}) all-reduce(f32[48,48]{1,0:T(8,128)S(1)} %convolution_bitcast_fusion.1, f32[48,48]{1,0:T(8,128)S(1)} %convolution_bitcast_fusion), channel_id=1, replica_groups=mesh['gx'=8,'gy'=8,'gz'=4] {'gx','gy','gz'}, use_global_device_ids=true, to_apply=%region_37.45 | all-reduce | flops 4608 | bytes 36864 | tf_op jit(solution)/shard_map/psum | solution.py:198
  679.4 4.4 cholesky.324
  686.1 4.4 cholesky.335
  691.8 3.7 custom-call.75
  720.1 3.7 custom-call.77
  (565 shorter events, 184.2 us)
Async XLA Ops:
  9.2 21.6 %collective-permute-start.1 = (f32[17,1,4,128]{3,0,2,1:T(8,128)S(1)}, f32[17,1,4,128]{3,0,2,1:T(8,128)S(1)}, u32[]{:S(2)}, u32[]{:S(2)}) collective-permute-start(f32[17,1,4,128]{3,0,2,1:T(8,128)S(1)} %get-tuple-element.60), channel_id=1, source_target_pairs={{32,0},{64,32},{96,64},{128,96},{160,128},{192,160},{224,192},{33,... | collective-permute-start | bytes 104456 | tf_op jit(solution)/shard_map/ppermute | solution.py:24
  10.5 20.3 %collective-permute-start = (f32[17,1,4,128]{3,0,2,1:T(8,128)S(1)}, f32[17,1,4,128]{3,0,2,1:T(8,128)S(1)}, u32[]{:S(2)}, u32[]{:S(2)}) collective-permute-start(f32[17,1,4,128]{3,0,2,1:T(8,128)S(1)} %get-tuple-element.59), channel_id=1, source_target_pairs={{0,32},{32,64},{64,96},{96,128},{128,160},{160,192},{192,224},{1,3... | collective-permute-start | bytes 104456 | tf_op jit(solution)/shard_map/ppermute | solution.py:23
  16.2 8.1 %collective-permute-start.31 = (f32[16,1,4,128]{3,0,2,1:T(8,128)S(1)}, f32[16,1,4,128]{3,0,2,1:T(8,128)S(1)}, u32[]{:S(2)}, u32[]{:S(2)}) collective-permute-start(f32[16,1,4,128]{3,0,2,1:T(8,128)S(1)} %get-tuple-element.72), channel_id=1, source_target_pairs={{0,32},{32,64},{64,96},{96,128},{128,160},{160,192},{192,224},{1,3... | collective-permute-start | bytes 98312 | tf_op jit(solution)/shard_map/ppermute | solution.py:23
  20.0 5.8 collective-permute-start.30
  26.4 9.5 %collective-permute-start.32 = (f32[16,10,1,128]{3,0,2,1:T(8,128)S(1)}, f32[16,10,1,128]{3,0,2,1:T(8,128)S(1)}, u32[]{:S(2)}, u32[]{:S(2)}) collective-permute-start(f32[16,10,1,128]{3,0,2,1:T(8,128)S(1)} %get-tuple-element.56), channel_id=1, source_target_pairs={{4,0},{8,4},{12,8},{16,12},{20,16},{24,20},{28,24},{5,1},{9,5},{13... | collective-permute-start | bytes 245768 | tf_op jit(solution)/shard_map/ppermute | solution.py:24
  28.4 7.6 %collective-permute-start.33 = (f32[16,10,1,128]{3,0,2,1:T(8,128)S(1)}, f32[16,10,1,128]{3,0,2,1:T(8,128)S(1)}, u32[]{:S(2)}, u32[]{:S(2)}) collective-permute-start(f32[16,10,1,128]{3,0,2,1:T(8,128)S(1)} %get-tuple-element.55), channel_id=1, source_target_pairs={{0,4},{4,8},{8,12},{12,16},{16,20},{20,24},{24,28},{1,5},{5,9},{9,... | collective-permute-start | bytes 245768 | tf_op jit(solution)/shard_map/ppermute | solution.py:23
  30.8 5.6 collective-permute-start.3
  34.0 6.2 collective-permute-start.2
  41.0 12.9 %collective-permute-start.4 = (f32[17,10,6,1]{0,3,2,1:T(1,128)S(1)}, f32[17,10,6,1]{0,3,2,1:T(1,128)S(1)}, u32[]{:S(2)}, u32[]{:S(2)}) collective-permute-start(f32[17,10,6,1]{0,3,2,1:T(1,128)S(1)} %copy.640), channel_id=1, source_target_pairs={{0,1},{1,2},{2,3},{4,5},{5,6},{6,7},{8,9},{9,10},{10,11},{12,13},{... | collective-permute-start | bytes 12248 | tf_op jit(solution)/shard_map/ppermute | solution.py:23
  44.9 9.5 %collective-permute-start.5 = (f32[17,10,6,1]{0,3,2,1:T(1,128)S(1)}, f32[17,10,6,1]{0,3,2,1:T(1,128)S(1)}, u32[]{:S(2)}, u32[]{:S(2)}) collective-permute-start(f32[17,10,6,1]{0,3,2,1:T(1,128)S(1)} %copy.641), channel_id=1, source_target_pairs={{1,0},{2,1},{3,2},{5,4},{6,5},{7,6},{9,8},{10,9},{11,10},{13,12},{... | collective-permute-start | bytes 12248 | tf_op jit(solution)/shard_map/ppermute | solution.py:24
  47.3 106.5 %collective-permute-start.35 = (f32[16,10,6,1]{3,0,2,1:T(8,128)}, f32[16,10,6,1]{3,0,2,1:T(8,128)}, u32[]{:S(2)}, u32[]{:S(2)}) collective-permute-start(f32[16,10,6,1]{3,0,2,1:T(8,128)} %get-tuple-element.44), channel_id=1, source_target_pairs={{0,1},{1,2},{2,3},{4,5},{5,6},{6,7},{8,9},{9,10},{10,11},{12,13},{... | collective-permute-start | bytes 11528 | tf_op jit(solution)/shard_map/ppermute | solution.py:23
  52.6 105.8 %collective-permute-start.34 = (f32[16,10,6,1]{3,0,2,1:T(8,128)}, f32[16,10,6,1]{3,0,2,1:T(8,128)}, u32[]{:S(2)}, u32[]{:S(2)}) collective-permute-start(f32[16,10,6,1]{3,0,2,1:T(8,128)} %get-tuple-element.43), channel_id=1, source_target_pairs={{1,0},{2,1},{3,2},{5,4},{6,5},{7,6},{9,8},{10,9},{11,10},{13,12},{... | collective-permute-start | bytes 11528 | tf_op jit(solution)/shard_map/ppermute | solution.py:24
  56.1 162.6 %copy-start.40 = (f32[4,2,64]{2,1,0:T(2,128)}, f32[4,2,64]{2,1,0:T(2,128)S(1)}, u32[]{:S(2)}) copy-start(f32[4,2,64]{2,1,0:T(2,128)S(1)} %get-tuple-element.116) | copy-start | bytes 6148
  56.1 162.6 %copy-start.42 = (f32[4,2,64]{2,1,0:T(2,128)}, f32[4,2,64]{2,1,0:T(2,128)S(1)}, u32[]{:S(2)}) copy-start(f32[4,2,64]{2,1,0:T(2,128)S(1)} %get-tuple-element.117) | copy-start | bytes 6148
  145.2 23.6 %collective-permute-start.12 = (f32[16,1,2,64]{0,3,2,1:T(8,128)}, f32[16,1,2,64]{0,3,2,1:T(8,128)S(1)}, u32[]{:S(2)}, u32[]{:S(2)}) collective-permute-start(f32[16,1,2,64]{0,3,2,1:T(8,128)} %get-tuple-element.78), channel_id=1, source_target_pairs={{32,0},{64,32},{96,64},{128,96},{160,128},{192,160},{224,192},{33,... | collective-permute-start | bytes 24584 | tf_op jit(solution)/shard_map/ppermute | solution.py:24
  146.5 24.8 %collective-permute-start.13 = (f32[16,1,2,64]{0,3,2,1:T(8,128)}, f32[16,1,2,64]{0,3,2,1:T(8,128)S(1)}, u32[]{:S(2)}, u32[]{:S(2)}) collective-permute-start(f32[16,1,2,64]{0,3,2,1:T(8,128)} %get-tuple-element.77), channel_id=1, source_target_pairs={{0,32},{32,64},{64,96},{96,128},{128,160},{160,192},{192,224},{1,3... | collective-permute-start | bytes 24584 | tf_op jit(solution)/shard_map/ppermute | solution.py:23
  152.5 9.8 %collective-permute-start.18 = (f32[16,1,1,32]{0,3,1,2:T(8,128)S(1)}, f32[16,1,1,32]{0,3,1,2:T(8,128)S(1)}, u32[]{:S(2)}, u32[]{:S(2)}) collective-permute-start(f32[16,1,1,32]{0,3,1,2:T(8,128)S(1)} %get-tuple-element.106), channel_id=1, source_target_pairs={{32,0},{64,32},{96,64},{128,96},{160,128},{192,160},{224,192},{33,... | collective-permute-start | bytes 6152 | tf_op jit(solution)/shard_map/ppermute | solution.py:24
  153.8 13.0 %collective-permute-start.19 = (f32[16,1,1,32]{0,3,1,2:T(8,128)S(1)}, f32[16,1,1,32]{0,3,1,2:T(8,128)S(1)}, u32[]{:S(2)}, u32[]{:S(2)}) collective-permute-start(f32[16,1,1,32]{0,3,1,2:T(8,128)S(1)} %get-tuple-element.105), channel_id=1, source_target_pairs={{0,32},{32,64},{64,96},{96,128},{128,160},{160,192},{192,224},{1,3... | collective-permute-start | bytes 6152 | tf_op jit(solution)/shard_map/ppermute | solution.py:23
  160.7 58.1 %copy-start.44 = (f32[4,2,64]{2,1,0:T(2,128)}, f32[4,2,64]{2,1,0:T(2,128)S(1)}, u32[]{:S(2)}) copy-start(f32[4,2,64]{2,1,0:T(2,128)S(1)} %copy.668) | copy-start | bytes 6148
  161.0 31.9 %collective-permute-start.6 = (f32[16,1,4,128]{3,0,2,1:T(8,128)S(1)}, f32[16,1,4,128]{3,0,2,1:T(8,128)S(1)}, u32[]{:S(2)}, u32[]{:S(2)}) collective-permute-start(f32[16,1,4,128]{3,0,2,1:T(8,128)S(1)} %get-tuple-element.74), channel_id=1, source_target_pairs={{32,0},{64,32},{96,64},{128,96},{160,128},{192,160},{224,192},{33,... | collective-permute-start | bytes 98312 | tf_op jit(solution)/shard_map/ppermute | solution.py:24
  162.3 30.6 %collective-permute-start.7 = (f32[16,1,4,128]{3,0,2,1:T(8,128)S(1)}, f32[16,1,4,128]{3,0,2,1:T(8,128)S(1)}, u32[]{:S(2)}, u32[]{:S(2)}) collective-permute-start(f32[16,1,4,128]{3,0,2,1:T(8,128)S(1)} %get-tuple-element.73), channel_id=1, source_target_pairs={{0,32},{32,64},{64,96},{96,128},{128,160},{160,192},{192,224},{1,3... | collective-permute-start | bytes 98312 | tf_op jit(solution)/shard_map/ppermute | solution.py:23
  166.9 4.5 collective-permute-start.20
  168.8 5.6 collective-permute-start.21
  174.4 5.7 collective-permute-start.23
  176.9 5.7 collective-permute-start.22
  178.2 5.2 collective-permute-start.14
  180.1 5.4 collective-permute-start.15
  186.3 22.3 %collective-permute-start.16 = (f32[16,6,4,1]{3,0,2,1:T(8,128)}, f32[16,6,4,1]{3,0,2,1:T(8,128)S(1)}, u32[]{:S(2)}, u32[]{:S(2)}) collective-permute-start(f32[16,6,4,1]{3,0,2,1:T(8,128)} %get-tuple-element.89), channel_id=1, source_target_pairs={{1,0},{2,1},{3,2},{5,4},{6,5},{7,6},{9,8},{10,9},{11,10},{13,12},{... | collective-permute-start | bytes 4616 | tf_op jit(solution)/shard_map/ppermute | solution.py:24
  187.6 21.0 %collective-permute-start.17 = (f32[16,6,4,1]{3,0,2,1:T(8,128)}, f32[16,6,4,1]{3,0,2,1:T(8,128)S(1)}, u32[]{:S(2)}, u32[]{:S(2)}) collective-permute-start(f32[16,6,4,1]{3,0,2,1:T(8,128)} %get-tuple-element.90), channel_id=1, source_target_pairs={{0,1},{1,2},{2,3},{4,5},{5,6},{6,7},{8,9},{9,10},{10,11},{12,13},{... | collective-permute-start | bytes 4616 | tf_op jit(solution)/shard_map/ppermute | solution.py:23
  193.7 15.5 %collective-permute-start.8 = (f32[16,10,1,128]{3,0,2,1:T(8,128)}, f32[16,10,1,128]{3,0,2,1:T(8,128)S(1)}, u32[]{:S(2)}, u32[]{:S(2)}) collective-permute-start(f32[16,10,1,128]{3,0,2,1:T(8,128)} %get-tuple-element.58), channel_id=1, source_target_pairs={{4,0},{8,4},{12,8},{16,12},{20,16},{24,20},{28,24},{5,1},{9,5},{13... | collective-permute-start | bytes 245768 | tf_op jit(solution)/shard_map/ppermute | solution.py:24
  195.6 14.3 %collective-permute-start.9 = (f32[16,10,1,128]{3,0,2,1:T(8,128)}, f32[16,10,1,128]{3,0,2,1:T(8,128)}, u32[]{:S(2)}, u32[]{:S(2)}) collective-permute-start(f32[16,10,1,128]{3,0,2,1:T(8,128)} %get-tuple-element.57), channel_id=1, source_target_pairs={{0,4},{4,8},{8,12},{12,16},{16,20},{20,24},{24,28},{1,5},{5,9},{9,... | collective-permute-start | bytes 245768 | tf_op jit(solution)/shard_map/ppermute | solution.py:23
  212.0 15.7 %collective-permute-start.11 = (f32[16,10,6,1]{3,0,2,1:T(8,128)}, f32[16,10,6,1]{3,0,2,1:T(8,128)}, u32[]{:S(2)}, u32[]{:S(2)}) collective-permute-start(f32[16,10,6,1]{3,0,2,1:T(8,128)} %get-tuple-element.46), channel_id=1, source_target_pairs={{0,1},{1,2},{2,3},{4,5},{5,6},{6,7},{8,9},{9,10},{10,11},{12,13},{... | collective-permute-start | bytes 11528 | tf_op jit(solution)/shard_map/ppermute | solution.py:23
  216.7 15.9 %collective-permute-start.10 = (f32[16,10,6,1]{3,0,2,1:T(8,128)}, f32[16,10,6,1]{3,0,2,1:T(8,128)}, u32[]{:S(2)}, u32[]{:S(2)}) collective-permute-start(f32[16,10,6,1]{3,0,2,1:T(8,128)} %get-tuple-element.45), channel_id=1, source_target_pairs={{1,0},{2,1},{3,2},{5,4},{6,5},{7,6},{9,8},{10,9},{11,10},{13,12},{... | collective-permute-start | bytes 11528 | tf_op jit(solution)/shard_map/ppermute | solution.py:24
  234.1 5.9 collective-permute-start.24
  235.4 6.1 collective-permute-start.25
  241.5 4.4 collective-permute-start.26
  243.5 5.8 collective-permute-start.27
  250.4 11.7 %collective-permute-start.29 = (f32[16,10,6,1]{3,0,2,1:T(8,128)}, f32[16,10,6,1]{3,0,2,1:T(8,128)}, u32[]{:S(2)}, u32[]{:S(2)}) collective-permute-start(f32[16,10,6,1]{3,0,2,1:T(8,128)} %get-tuple-element.42), channel_id=1, source_target_pairs={{0,1},{1,2},{2,3},{4,5},{5,6},{6,7},{8,9},{9,10},{10,11},{12,13},{... | collective-permute-start | bytes 11528 | tf_op jit(solution)/shard_map/ppermute | solution.py:23
  252.8 14.1 %collective-permute-start.28 = (f32[16,10,6,1]{3,0,2,1:T(8,128)}, f32[16,10,6,1]{3,0,2,1:T(8,128)}, u32[]{:S(2)}, u32[]{:S(2)}) collective-permute-start(f32[16,10,6,1]{3,0,2,1:T(8,128)} %get-tuple-element.41), channel_id=1, source_target_pairs={{1,0},{2,1},{3,2},{5,4},{6,5},{7,6},{9,8},{10,9},{11,10},{13,12},{... | collective-permute-start | bytes 11528 | tf_op jit(solution)/shard_map/ppermute | solution.py:24
  268.4 85.1 %copy-start.5 = (f32[16,8,4,128]{3,0,2,1:T(8,128)}, f32[16,8,4,128]{3,0,2,1:T(8,128)S(1)}, u32[]{:S(2)}) copy-start(f32[16,8,4,128]{3,0,2,1:T(8,128)S(1)} %fusion.68) | copy-start | bytes 786436
  481.3 25.3 %collective-permute-start.42 = (f32[16,1,2,64]{0,3,2,1:T(8,128)}, f32[16,1,2,64]{0,3,2,1:T(8,128)}, u32[]{:S(2)}, u32[]{:S(2)}) collective-permute-start(f32[16,1,2,64]{0,3,2,1:T(8,128)} %get-tuple-element.68), channel_id=1, source_target_pairs={{32,0},{64,32},{96,64},{128,96},{160,128},{192,160},{224,192},{33,... | collective-permute-start | bytes 24584 | tf_op jit(solution)/shard_map/ppermute | solution.py:24
  482.6 27.4 %collective-permute-start.43 = (f32[16,1,2,64]{0,3,2,1:T(8,128)}, f32[16,1,2,64]{0,3,2,1:T(8,128)}, u32[]{:S(2)}, u32[]{:S(2)}) collective-permute-start(f32[16,1,2,64]{0,3,2,1:T(8,128)} %get-tuple-element.67), channel_id=1, source_target_pairs={{0,32},{32,64},{64,96},{96,128},{128,160},{160,192},{192,224},{1,3... | collective-permute-start | bytes 24584 | tf_op jit(solution)/shard_map/ppermute | solution.py:23
  488.4 11.7 %collective-permute-start.48 = (f32[16,1,1,32]{0,3,1,2:T(8,128)S(1)}, f32[16,1,1,32]{0,3,1,2:T(8,128)S(1)}, u32[]{:S(2)}, u32[]{:S(2)}) collective-permute-start(f32[16,1,1,32]{0,3,1,2:T(8,128)S(1)} %get-tuple-element.104), channel_id=1, source_target_pairs={{32,0},{64,32},{96,64},{128,96},{160,128},{192,160},{224,192},{33,... | collective-permute-start | bytes 6152 | tf_op jit(solution)/shard_map/ppermute | solution.py:24
  489.7 14.9 %collective-permute-start.49 = (f32[16,1,1,32]{0,3,1,2:T(8,128)S(1)}, f32[16,1,1,32]{0,3,1,2:T(8,128)S(1)}, u32[]{:S(2)}, u32[]{:S(2)}) collective-permute-start(f32[16,1,1,32]{0,3,1,2:T(8,128)S(1)} %get-tuple-element.103), channel_id=1, source_target_pairs={{0,32},{32,64},{64,96},{96,128},{128,160},{160,192},{192,224},{1,3... | collective-permute-start | bytes 6152 | tf_op jit(solution)/shard_map/ppermute | solution.py:23
  497.9 23.2 %collective-permute-start.36 = (f32[16,1,4,128]{3,0,2,1:T(8,128)S(1)}, f32[16,1,4,128]{3,0,2,1:T(8,128)S(1)}, u32[]{:S(2)}, u32[]{:S(2)}) collective-permute-start(f32[16,1,4,128]{3,0,2,1:T(8,128)S(1)} %get-tuple-element.66), channel_id=1, source_target_pairs={{32,0},{64,32},{96,64},{128,96},{160,128},{192,160},{224,192},{33,... | collective-permute-start | bytes 98312 | tf_op jit(solution)/shard_map/ppermute | solution.py:24
  500.1 21.0 %collective-permute-start.37 = (f32[16,1,4,128]{3,0,2,1:T(8,128)S(1)}, f32[16,1,4,128]{3,0,2,1:T(8,128)S(1)}, u32[]{:S(2)}, u32[]{:S(2)}) collective-permute-start(f32[16,1,4,128]{3,0,2,1:T(8,128)S(1)} %get-tuple-element.65), channel_id=1, source_target_pairs={{0,32},{32,64},{64,96},{96,128},{128,160},{160,192},{192,224},{1,3... | collective-permute-start | bytes 98312 | tf_op jit(solution)/shard_map/ppermute | solution.py:23
  504.7 6.2 collective-permute-start.50
  506.6 5.7 collective-permute-start.51
  512.4 5.5 collective-permute-start.53
  514.6 5.7 collective-permute-start.52
  515.9 11.0 %collective-permute-start.44 = (f32[16,6,1,64]{3,0,2,1:T(8,128)S(1)}, f32[16,6,1,64]{3,0,2,1:T(8,128)S(1)}, u32[]{:S(2)}, u32[]{:S(2)}) collective-permute-start(f32[16,6,1,64]{3,0,2,1:T(8,128)S(1)} %get-tuple-element.94), channel_id=1, source_target_pairs={{4,0},{8,4},{12,8},{16,12},{20,16},{24,20},{28,24},{5,1},{9,5},{13... | collective-permute-start | bytes 73736 | tf_op jit(solution)/shard_map/ppermute | solution.py:24
  517.9 9.0 %collective-permute-start.45 = (f32[16,6,1,64]{3,0,2,1:T(8,128)S(1)}, f32[16,6,1,64]{3,0,2,1:T(8,128)S(1)}, u32[]{:S(2)}, u32[]{:S(2)}) collective-permute-start(f32[16,6,1,64]{3,0,2,1:T(8,128)S(1)} %get-tuple-element.93), channel_id=1, source_target_pairs={{0,4},{4,8},{8,12},{12,16},{16,20},{20,24},{24,28},{1,5},{5,9},{9,... | collective-permute-start | bytes 73736 | tf_op jit(solution)/shard_map/ppermute | solution.py:23
  521.8 17.4 %collective-permute-start.38 = (f32[16,10,1,128]{3,0,2,1:T(8,128)}, f32[16,10,1,128]{3,0,2,1:T(8,128)}, u32[]{:S(2)}, u32[]{:S(2)}) collective-permute-start(f32[16,10,1,128]{3,0,2,1:T(8,128)} %get-tuple-element.52), channel_id=1, source_target_pairs={{4,0},{8,4},{12,8},{16,12},{20,16},{24,20},{28,24},{5,1},{9,5},{13... | collective-permute-start | bytes 245768 | tf_op jit(solution)/shard_map/ppermute | solution.py:24
  525.0 14.2 %collective-permute-start.39 = (f32[16,10,1,128]{3,0,2,1:T(8,128)}, f32[16,10,1,128]{3,0,2,1:T(8,128)}, u32[]{:S(2)}, u32[]{:S(2)}) collective-permute-start(f32[16,10,1,128]{3,0,2,1:T(8,128)} %get-tuple-element.51), channel_id=1, source_target_pairs={{0,4},{4,8},{8,12},{12,16},{16,20},{20,24},{24,28},{1,5},{5,9},{9,... | collective-permute-start | bytes 245768 | tf_op jit(solution)/shard_map/ppermute | solution.py:23
  527.1 9.8 %collective-permute-start.46 = (f32[16,6,4,1]{3,0,2,1:T(8,128)S(1)}, f32[16,6,4,1]{3,0,2,1:T(8,128)S(1)}, u32[]{:S(2)}, u32[]{:S(2)}) collective-permute-start(f32[16,6,4,1]{3,0,2,1:T(8,128)S(1)} %get-tuple-element.83), channel_id=1, source_target_pairs={{1,0},{2,1},{3,2},{5,4},{6,5},{7,6},{9,8},{10,9},{11,10},{13,12},{... | collective-permute-start | bytes 4616 | tf_op jit(solution)/shard_map/ppermute | solution.py:24
  528.4 10.2 %collective-permute-start.47 = (f32[16,6,4,1]{3,0,2,1:T(8,128)S(1)}, f32[16,6,4,1]{3,0,2,1:T(8,128)S(1)}, u32[]{:S(2)}, u32[]{:S(2)}) collective-permute-start(f32[16,6,4,1]{3,0,2,1:T(8,128)S(1)} %get-tuple-element.84), channel_id=1, source_target_pairs={{0,1},{1,2},{2,3},{4,5},{5,6},{6,7},{8,9},{9,10},{10,11},{12,13},{... | collective-permute-start | bytes 4616 | tf_op jit(solution)/shard_map/ppermute | solution.py:23
  541.4 15.4 %collective-permute-start.41 = (f32[16,10,6,1]{3,0,2,1:T(8,128)}, f32[16,10,6,1]{3,0,2,1:T(8,128)}, u32[]{:S(2)}, u32[]{:S(2)}) collective-permute-start(f32[16,10,6,1]{3,0,2,1:T(8,128)} %get-tuple-element.40), channel_id=1, source_target_pairs={{0,1},{1,2},{2,3},{4,5},{5,6},{6,7},{8,9},{9,10},{10,11},{12,13},{... | collective-permute-start | bytes 11528 | tf_op jit(solution)/shard_map/ppermute | solution.py:23
  546.5 15.2 %collective-permute-start.40 = (f32[16,10,6,1]{3,0,2,1:T(8,128)}, f32[16,10,6,1]{3,0,2,1:T(8,128)}, u32[]{:S(2)}, u32[]{:S(2)}) collective-permute-start(f32[16,10,6,1]{3,0,2,1:T(8,128)} %get-tuple-element.39), channel_id=1, source_target_pairs={{1,0},{2,1},{3,2},{5,4},{6,5},{7,6},{9,8},{10,9},{11,10},{13,12},{... | collective-permute-start | bytes 11528 | tf_op jit(solution)/shard_map/ppermute | solution.py:24
  563.7 5.9 collective-permute-start.54
  565.0 6.1 collective-permute-start.55
  571.2 4.7 collective-permute-start.56
  573.4 5.8 collective-permute-start.57
  580.3 12.9 %collective-permute-start.59 = (f32[16,10,6,1]{3,0,2,1:T(8,128)}, f32[16,10,6,1]{3,0,2,1:T(8,128)}, u32[]{:S(2)}, u32[]{:S(2)}) collective-permute-start(f32[16,10,6,1]{3,0,2,1:T(8,128)} %get-tuple-element.38), channel_id=1, source_target_pairs={{0,1},{1,2},{2,3},{4,5},{5,6},{6,7},{8,9},{9,10},{10,11},{12,13},{... | collective-permute-start | bytes 11528 | tf_op jit(solution)/shard_map/ppermute | solution.py:23
  584.4 13.7 %collective-permute-start.58 = (f32[16,10,6,1]{3,0,2,1:T(8,128)}, f32[16,10,6,1]{3,0,2,1:T(8,128)}, u32[]{:S(2)}, u32[]{:S(2)}) collective-permute-start(f32[16,10,6,1]{3,0,2,1:T(8,128)} %get-tuple-element.37), channel_id=1, source_target_pairs={{1,0},{2,1},{3,2},{5,4},{6,5},{7,6},{9,8},{10,9},{11,10},{13,12},{... | collective-permute-start | bytes 11528 | tf_op jit(solution)/shard_map/ppermute | solution.py:24
  (64 other events, 1093.4 us)
where the time goes:
time: 736 us; the launch traced here: 727 us
  blocking collectives  309 us (42%)
  starting transfers between devices  167 us (23%)
  other arithmetic  106 us (14%)
  waiting for transfers between devices  65.1 us (9%)
  local copies, waits for them, and re-layouts  43.5 us (6%)
  matrix products  33 us (4%)
    psum x2, blocking collectives, on_device(): lax.psum((matmul_high(flat_x, flat_x.T), matmul_high(flat_x, flat_ax.T)),...  156 us
    psum x2, blocking collectives, on_device(): lax.psum((matmul_high(search, search.T), matmul_high(search, applied.T)),...  153 us
    ppermute x30, starting transfers between devices, with_halo(): before = lax.ppermute(last, axis, up)  119 us
    ppermute x30, starting transfers between devices, with_halo(): after = lax.ppermute(leading, axis, down)  47.7 us
    ppermute x30, waiting for transfers between devices, with_halo(): before = lax.ppermute(last, axis, up)  40.6 us
    dot_general x40, matrix products, matmul_high(): return jnp.dot(first_side, second_side, precision=lax.Precision.HIGHEST)  27.9 us
    ppermute x30, waiting for transfers between devices, with_halo(): after = lax.ppermute(leading, axis, down)  24.5 us
    another operation x24, other arithmetic, ritz_step(): small_factor = jnp.linalg.cholesky(matmul_high(mapped.T, mapped))  17.5 us
  transfers between devices with their start and end apart: 60, of which 20 were waited for; matrix products, arithmetic and copies ran while one was open for 7% of the time, Pallas kernels for 0%

commit v1 on v0

--- a/solution.py
+++ b/solution.py
@@ -157,6 +157,15 @@
 
 def coarse_rim(field):
     return with_halo(field, (("gx", 1), ("gy", 2), ("gz", 3)), 1)
+
+
+def all_sum(values):
+    for axis, bit in (
+        ("gy", 1), ("gx", 1), ("gz", 1), ("gy", 2), ("gx", 2), ("gz", 2), ("gy", 4), ("gx", 4),
+    ):
+        peers = lax.axis_size(axis)
+        values = values + lax.ppermute(values, axis, [(i, i ^ bit) for i in range(peers)])
+    return values
 
 
 def on_device(x_block, p_block, voxel_class, conductance):
@@ -186,19 +195,23 @@
     for iteration in range(ITERS):
         flat_x = block_x.reshape(VECS, -1)
         flat_ax = applied_x.reshape(VECS, -1)
-        gram_x, cross_x = lax.psum(
-            (matmul_high(flat_x, flat_x.T), matmul_high(flat_x, flat_ax.T)), ("gx", "gy", "gz")
-        )
-        projected = solve_small(gram_x / all_cells, cross_x / all_cells)
+        if iteration == 0:
+            pair = jnp.concatenate([matmul_high(flat_x, flat_x.T), matmul_high(flat_x, flat_ax.T)], 0)
+            pair = all_sum(pair.reshape(4, 128)).reshape(2 * VECS, VECS) / all_cells
+            gram_x, cross_x = pair[:VECS], pair[VECS:]
+        else:
+            gram_x = matmul_high(coefficients.T, matmul_high(gram_b, coefficients))
+            cross_x = matmul_high(coefficients.T, matmul_high(gram_a, coefficients))
+        projected = solve_small(gram_x, cross_x)
         residual = applied_x - matmul_high(projected.T, flat_x).reshape(block_x.shape)
         block_w = precondition(residual, levels, rims)
         applied_w = apply_operator(fine_rim(block_w), block_w, levels[0][0], levels[0][1])
         search = jnp.concatenate([block_x, block_w, block_p], 0).reshape(3 * VECS, -1)
         applied = jnp.concatenate([applied_x, applied_w, applied_p], 0).reshape(3 * VECS, -1)
-        gram_b, gram_a = lax.psum(
-            (matmul_high(search, search.T), matmul_high(search, applied.T)), ("gx", "gy", "gz")
-        )
-        coefficients, rayleigh = ritz_step(gram_b / all_cells, gram_a / all_cells, VECS, INNER)
+        pair = jnp.concatenate([matmul_high(search, search.T), matmul_high(search, applied.T)], 0)
+        pair = all_sum(pair.reshape(36, 128)).reshape(6 * VECS, 3 * VECS) / all_cells
+        gram_b, gram_a = pair[: 3 * VECS], pair[3 * VECS :]
+        coefficients, rayleigh = ritz_step(gram_b, gram_a, VECS, INNER)
         tail = coefficients[VECS:]
         block_x = matmul_high(coefficients.T, search).reshape(x_block.shape)
         applied_x = matmul_high(coefficients.T, applied).reshape(x_block.shape)

time: 736 us -> 523 us (0.71)
  blocking collectives: 309 us -> 0 us
  waiting for transfers between devices: 65.1 us -> 123 us
  starting transfers between devices: 167 us -> 212 us
    psum x4 -> x0, blocking collectives: 309 us -> none  [the longest x2 156 us: on_device(): lax.psum((matmul_high(flat_x, flat_x.T), matmul_high(flat_x, flat_ax.T)),...]
    ppermute x0 -> x24, starting transfers between devices: none -> 60.1 us  [all_sum(): lax.ppermute(values, axis, [(i, i ^ bit) for i in range(peers)])]
    ppermute x0 -> x24, waiting for transfers between devices: none -> 51.6 us  [all_sum(): lax.ppermute(values, axis, [(i, i ^ bit) for i in range(peers)])]
    ppermute x30, starting transfers between devices: 119 us -> 106 us  [with_halo(): before = lax.ppermute(last, axis, up)]
    dot_general x40 -> x42, matrix products: 27.9 us -> 26.6 us  [matmul_high(): return jnp.dot(first_side, second_side, precision=lax.Precision.HIGHEST)]
  transfers between devices with their start and end apart: 60 -> 84, of which waited for: 20 -> 42; matrix products, arithmetic and copies ran while one was open for 7% -> 8% of each run, Pallas kernels for 0% -> 0%
where the time goes in v1:
time: 523 us; the launch traced here: 512 us
  starting transfers between devices  212 us (41%)
  waiting for transfers between devices  123 us (24%)
  other arithmetic  101 us (19%)
  local copies, waits for them, and re-layouts  39.9 us (8%)
  matrix products  31.8 us (6%)
    ppermute x30, starting transfers between devices, with_halo(): before = lax.ppermute(last, axis, up)  106 us
    ppermute x24, starting transfers between devices, all_sum(): lax.ppermute(values, axis, [(i, i ^ bit) for i in range(peers)])  60.1 us
    ppermute x24, waiting for transfers between devices, all_sum(): lax.ppermute(values, axis, [(i, i ^ bit) for i in range(peers)])  51.6 us
    ppermute x30, starting transfers between devices, with_halo(): after = lax.ppermute(leading, axis, down)  46.2 us
    ppermute x30, waiting for transfers between devices, with_halo(): before = lax.ppermute(last, axis, up)  44.6 us
    ppermute x30, waiting for transfers between devices, with_halo(): after = lax.ppermute(leading, axis, down)  27 us
    dot_general x42, matrix products, matmul_high(): return jnp.dot(first_side, second_side, precision=lax.Precision.HIGHEST)  26.6 us
    another operation x24, other arithmetic, ritz_step(): small_factor = jnp.linalg.cholesky(matmul_high(mapped.T, mapped))  17.2 us
  transfers between devices with their start and end apart: 84, of which 42 were waited for; matrix products, arithmetic and copies ran while one was open for 8% of the time, Pallas kernels for 0%

profile of v1, /device:TPU:8, one launch (start us, length us, event | category | flops | bytes accessed | tf_op | source)
XLA Modules:
  0.0 512.5 jit_solution(10961620095651135032)
XLA Ops:
  3.4 5.8 %select_add_fusion = f32[8,4,128]{2,1,0:T(4,128)S(1)} fusion(s32[8,4,128]{2,1,0:T(4,128)} %param.18, f32[]{:T(128)} %bitcast.7, f32[]{:T(128)} %bitcast.6, f32[]{:T(128)} %bitcast.5, f32[]{:T(128)} %bitcast.4, f32[]{:T(128)} %bitcast.3, f32[]{:T(128)} %bitcast.2, f32[]{:T(128)} %bitcast.1, f32[]{:T(128)} %bitcast), kind=kLoop, calls=%fused_computation.482 | loop fusion | flops 94208 | bytes 32800 | tf_op jit(solution)/shard_map/add | solution.py:176
  10.6 4.5 collective-permute-start
  16.3 3.8 collective-permute-start.39
  30.4 3.2 collective-permute-start.40
  36.3 3.4 collective-permute-start.4
  42.0 4.0 collective-permute-done.5
  51.6 3.0 collective-permute-start.7
  60.5 2.9 collective-permute-done.9
  63.4 4.6 collective-permute-start.10
  69.6 2.7 collective-permute-start.11
  79.8 6.0 %collective-permute-start.13 = (f32[4,128]{1,0:T(4,128)S(1)}, f32[4,128]{1,0:T(4,128)S(1)}, u32[]{:S(2)}, u32[]{:S(2)}) collective-permute-start(f32[4,128]{1,0:T(4,128)S(1)} %add.419), channel_id=1, source_target_pairs={{0,128},{32,160},{64,192},{96,224},{128,0},{160,32},{192,64},{224,... | collective-permute-start | bytes 6152 | tf_op jit(solution)/shard_map/ppermute | solution.py:167
  95.2 4.5 collective-permute-start.21
  101.8 4.5 collective-permute-start.27
  107.7 4.6 collective-permute-start.15
  114.2 2.4 collective-permute-start.29
  116.8 3.0 collective-permute-done.29
  119.8 3.4 collective-permute-start.31
  126.5 2.4 collective-permute-start.23
  134.0 5.9 %collective-permute-start.25 = (f32[16,6,4,1]{3,0,2,1:T(8,128)}, f32[16,6,4,1]{3,0,2,1:T(8,128)}, u32[]{:S(2)}, u32[]{:S(2)}) collective-permute-start(f32[16,6,4,1]{3,0,2,1:T(8,128)} %get-tuple-element.80), channel_id=1, source_target_pairs={{0,1},{1,2},{2,3},{4,5},{5,6},{6,7},{8,9},{9,10},{10,11},{12,13},{... | collective-permute-start | bytes 4616 | tf_op jit(solution)/shard_map/ppermute | solution.py:23
  150.6 4.0 collective-permute-start.19
  159.7 5.9 %collective-permute-done.19 = f32[16,10,6,1]{3,0,2,1:T(8,128)} collective-permute-done((f32[16,10,6,1]{3,0,2,1:T(8,128)}, f32[16,10,6,1]{3,0,2,1:T(8,128)}, u32[]{:S(2)}, u32[]{:S(2)}) %collective-permute-start.19) | collective-permute-done | bytes 3872 | tf_op jit(solution)/shard_map/ppermute | solution.py:23
  165.6 4.9 collective-permute-done.18
  173.4 5.2 %collective-permute-start.33 = (f32[16,1,4,128]{3,0,2,1:T(8,128)S(1)}, f32[16,1,4,128]{3,0,2,1:T(8,128)S(1)}, u32[]{:S(2)}, u32[]{:S(2)}) collective-permute-start(f32[16,1,4,128]{3,0,2,1:T(8,128)S(1)} %get-tuple-element.59), channel_id=1, source_target_pairs={{0,32},{32,64},{64,96},{96,128},{128,160},{160,192},{192,224},{1,3... | collective-permute-start | bytes 98312 | tf_op jit(solution)/shard_map/ppermute | solution.py:23
  184.4 2.4 collective-permute-start.35
  186.9 4.3 collective-permute-done.43
  191.1 4.1 collective-permute-done.42
  200.2 6.8 %collective-permute-done.37 = f32[16,10,6,1]{3,0,2,1:T(8,128)S(1)} collective-permute-done((f32[16,10,6,1]{3,0,2,1:T(8,128)S(1)}, f32[16,10,6,1]{3,0,2,1:T(8,128)S(1)}, u32[]{:S(2)}, u32[]{:S(2)}) %collective-permute-start.37) | collective-permute-done | bytes 3872 | tf_op jit(solution)/shard_map/ppermute | solution.py:23
  207.0 4.1 collective-permute-done.36
  213.8 3.2 collective-permute-start.45
  219.0 3.5 collective-permute-done.46
  222.8 3.6 collective-permute-done.47
  226.3 5.3 %collective-permute-start.48 = (f32[36,128]{1,0:T(8,128)S(1)}, f32[36,128]{1,0:T(8,128)S(1)}, u32[]{:S(2)}, u32[]{:S(2)}) collective-permute-start(f32[36,128]{1,0:T(8,128)S(1)} %add.469), channel_id=1, source_target_pairs={{0,64},{32,96},{64,0},{96,32},{128,192},{160,224},{192,128},{224,1... | collective-permute-start | bytes 55304 | tf_op jit(solution)/shard_map/ppermute | solution.py:167
  238.8 5.2 %collective-permute-done.50 = f32[36,128]{1,0:T(8,128)S(1)} collective-permute-done((f32[36,128]{1,0:T(8,128)S(1)}, f32[36,128]{1,0:T(8,128)S(1)}, u32[]{:S(2)}, u32[]{:S(2)}) %collective-permute-start.50) | collective-permute-done | bytes 18464 | tf_op jit(solution)/shard_map/ppermute | solution.py:167
  244.0 12.9 %collective-permute-start.51 = (f32[36,128]{1,0:T(8,128)S(1)}, f32[36,128]{1,0:T(8,128)S(1)}, u32[]{:S(2)}, u32[]{:S(2)}) collective-permute-start(f32[36,128]{1,0:T(8,128)S(1)} %add.472), channel_id=1, source_target_pairs={{0,128},{32,160},{64,192},{96,224},{128,0},{160,32},{192,64},{224,... | collective-permute-start | bytes 55304 | tf_op jit(solution)/shard_map/ppermute | solution.py:167
  263.3 4.4 cholesky.247
  269.8 4.4 cholesky.258
  275.5 3.7 custom-call.60
  303.9 3.7 custom-call.62
  318.2 4.5 collective-permute-start.59
  324.8 4.5 collective-permute-start.65
  330.7 4.5 collective-permute-start.53
  339.8 3.0 collective-permute-done.67
  348.2 2.6 collective-permute-start.61
  351.1 2.6 collective-permute-done.61
  355.1 5.5 %collective-permute-start.63 = (f32[16,6,4,1]{3,0,2,1:T(8,128)S(1)}, f32[16,6,4,1]{3,0,2,1:T(8,128)S(1)}, u32[]{:S(2)}, u32[]{:S(2)}) collective-permute-start(f32[16,6,4,1]{3,0,2,1:T(8,128)S(1)} %get-tuple-element.74), channel_id=1, source_target_pairs={{0,1},{1,2},{2,3},{4,5},{5,6},{6,7},{8,9},{9,10},{10,11},{12,13},{... | collective-permute-start | bytes 4616 | tf_op jit(solution)/shard_map/ppermute | solution.py:23
  365.7 2.8 collective-permute-done.55
  369.6 4.7 collective-permute-start.57
  378.5 4.1 collective-permute-done.57
  382.6 4.9 collective-permute-done.56
  390.3 4.5 collective-permute-start.71
  404.4 3.2 collective-permute-start.75
  409.7 7.0 %collective-permute-done.75 = f32[16,10,6,1]{3,0,2,1:T(8,128)S(1)} collective-permute-done((f32[16,10,6,1]{3,0,2,1:T(8,128)S(1)}, f32[16,10,6,1]{3,0,2,1:T(8,128)S(1)}, u32[]{:S(2)}, u32[]{:S(2)}) %collective-permute-start.75) | collective-permute-done | bytes 3872 | tf_op jit(solution)/shard_map/ppermute | solution.py:23
  416.6 4.1 collective-permute-done.74
  423.5 2.4 collective-permute-start.77
  427.9 3.5 collective-permute-done.78
  431.4 3.8 collective-permute-done.79
  435.2 5.9 %collective-permute-start.80 = (f32[36,128]{1,0:T(8,128)S(1)}, f32[36,128]{1,0:T(8,128)S(1)}, u32[]{:S(2)}, u32[]{:S(2)}) collective-permute-start(f32[36,128]{1,0:T(8,128)S(1)} %add.504), channel_id=1, source_target_pairs={{0,64},{32,96},{64,0},{96,32},{128,192},{160,224},{192,128},{224,1... | collective-permute-start | bytes 55304 | tf_op jit(solution)/shard_map/ppermute | solution.py:167
  443.9 4.2 collective-permute-done.81
  448.2 5.2 %collective-permute-done.82 = f32[36,128]{1,0:T(8,128)S(1)} collective-permute-done((f32[36,128]{1,0:T(8,128)S(1)}, f32[36,128]{1,0:T(8,128)S(1)}, u32[]{:S(2)}, u32[]{:S(2)}) %collective-permute-start.82) | collective-permute-done | bytes 18464 | tf_op jit(solution)/shard_map/ppermute | solution.py:167
  453.4 7.6 %collective-permute-start.83 = (f32[36,128]{1,0:T(8,128)S(1)}, f32[36,128]{1,0:T(8,128)S(1)}, u32[]{:S(2)}, u32[]{:S(2)}) collective-permute-start(f32[36,128]{1,0:T(8,128)S(1)} %add.507), channel_id=1, source_target_pairs={{0,128},{32,160},{64,192},{96,224},{128,0},{160,32},{192,64},{224,... | collective-permute-start | bytes 55304 | tf_op jit(solution)/shard_map/ppermute | solution.py:167
  464.2 4.4 cholesky.324
  470.9 4.4 cholesky.335
  476.6 3.7 custom-call.75
  505.0 3.7 custom-call.77
  (621 shorter events, 231.0 us)
Async XLA Ops:
  9.3 16.6 %collective-permute-start.1 = (f32[17,1,4,128]{3,0,2,1:T(8,128)S(1)}, f32[17,1,4,128]{3,0,2,1:T(8,128)S(1)}, u32[]{:S(2)}, u32[]{:S(2)}) collective-permute-start(f32[17,1,4,128]{3,0,2,1:T(8,128)S(1)} %get-tuple-element.52), channel_id=1, source_target_pairs={{32,0},{64,32},{96,64},{128,96},{160,128},{192,160},{224,192},{33,... | collective-permute-start | bytes 104456 | tf_op jit(solution)/shard_map/ppermute | solution.py:24
  10.6 15.4 %collective-permute-start = (f32[17,1,4,128]{3,0,2,1:T(8,128)S(1)}, f32[17,1,4,128]{3,0,2,1:T(8,128)S(1)}, u32[]{:S(2)}, u32[]{:S(2)}) collective-permute-start(f32[17,1,4,128]{3,0,2,1:T(8,128)S(1)} %get-tuple-element.51), channel_id=1, source_target_pairs={{0,32},{32,64},{64,96},{96,128},{128,160},{160,192},{192,224},{1,3... | collective-permute-start | bytes 104456 | tf_op jit(solution)/shard_map/ppermute | solution.py:23
  16.3 8.8 %collective-permute-start.39 = (f32[16,1,4,128]{3,0,2,1:T(8,128)S(1)}, f32[16,1,4,128]{3,0,2,1:T(8,128)S(1)}, u32[]{:S(2)}, u32[]{:S(2)}) collective-permute-start(f32[16,1,4,128]{3,0,2,1:T(8,128)S(1)} %get-tuple-element.62), channel_id=1, source_target_pairs={{0,32},{32,64},{64,96},{96,128},{128,160},{160,192},{192,224},{1,3... | collective-permute-start | bytes 98312 | tf_op jit(solution)/shard_map/ppermute | solution.py:23
  20.1 5.8 %collective-permute-start.38 = (f32[16,1,4,128]{3,0,2,1:T(8,128)S(1)}, f32[16,1,4,128]{3,0,2,1:T(8,128)S(1)}, u32[]{:S(2)}, u32[]{:S(2)}) collective-permute-start(f32[16,1,4,128]{3,0,2,1:T(8,128)S(1)} %get-tuple-element.61), channel_id=1, source_target_pairs={{32,0},{64,32},{96,64},{128,96},{160,128},{192,160},{224,192},{33,... | collective-permute-start | bytes 98312 | tf_op jit(solution)/shard_map/ppermute | solution.py:24
  26.0 9.5 %collective-permute-start.3 = (f32[17,10,1,128]{3,0,2,1:T(8,128)S(1)}, f32[17,10,1,128]{3,0,2,1:T(8,128)S(1)}, u32[]{:S(2)}, u32[]{:S(2)}) collective-permute-start(f32[17,10,1,128]{3,0,2,1:T(8,128)S(1)} %get-tuple-element.40), channel_id=1, source_target_pairs={{4,0},{8,4},{12,8},{16,12},{20,16},{24,20},{28,24},{5,1},{9,5},{13... | collective-permute-start | bytes 261128 | tf_op jit(solution)/shard_map/ppermute | solution.py:24
  27.9 7.5 %collective-permute-start.2 = (f32[17,10,1,128]{3,0,2,1:T(8,128)S(1)}, f32[17,10,1,128]{3,0,2,1:T(8,128)S(1)}, u32[]{:S(2)}, u32[]{:S(2)}) collective-permute-start(f32[17,10,1,128]{3,0,2,1:T(8,128)S(1)} %get-tuple-element.39), channel_id=1, source_target_pairs={{0,4},{4,8},{8,12},{12,16},{16,20},{20,24},{24,28},{1,5},{5,9},{9,... | collective-permute-start | bytes 261128 | tf_op jit(solution)/shard_map/ppermute | solution.py:23
  30.4 11.1 %collective-permute-start.40 = (f32[16,10,1,128]{3,0,2,1:T(8,128)S(1)}, f32[16,10,1,128]{3,0,2,1:T(8,128)S(1)}, u32[]{:S(2)}, u32[]{:S(2)}) collective-permute-start(f32[16,10,1,128]{3,0,2,1:T(8,128)S(1)} %get-tuple-element.48), channel_id=1, source_target_pairs={{4,0},{8,4},{12,8},{16,12},{20,16},{24,20},{28,24},{5,1},{9,5},{13... | collective-permute-start | bytes 245768 | tf_op jit(solution)/shard_map/ppermute | solution.py:24
  33.5 7.9 %collective-permute-start.41 = (f32[16,10,1,128]{3,0,2,1:T(8,128)S(1)}, f32[16,10,1,128]{3,0,2,1:T(8,128)S(1)}, u32[]{:S(2)}, u32[]{:S(2)}) collective-permute-start(f32[16,10,1,128]{3,0,2,1:T(8,128)S(1)} %get-tuple-element.47), channel_id=1, source_target_pairs={{0,4},{4,8},{8,12},{12,16},{16,20},{20,24},{24,28},{1,5},{5,9},{9,... | collective-permute-start | bytes 245768 | tf_op jit(solution)/shard_map/ppermute | solution.py:23
  40.1 5.9 %collective-permute-start.5 = (f32[17,10,6,1]{0,3,2,1:T(1,128)S(1)}, f32[17,10,6,1]{0,3,2,1:T(1,128)}, u32[]{:S(2)}, u32[]{:S(2)}) collective-permute-start(f32[17,10,6,1]{0,3,2,1:T(1,128)S(1)} %copy.587), channel_id=1, source_target_pairs={{1,0},{2,1},{3,2},{5,4},{6,5},{7,6},{9,8},{10,9},{11,10},{13,12},{... | collective-permute-start | bytes 12248 | tf_op jit(solution)/shard_map/ppermute | solution.py:24
  63.4 6.1 %collective-permute-start.10 = (f32[4,128]{1,0:T(4,128)S(1)}, f32[4,128]{1,0:T(4,128)S(1)}, u32[]{:S(2)}, u32[]{:S(2)}) collective-permute-start(f32[4,128]{1,0:T(4,128)S(1)} %add.416), channel_id=1, source_target_pairs={{0,64},{32,96},{64,0},{96,32},{128,192},{160,224},{192,128},{224,1... | collective-permute-start | bytes 6152 | tf_op jit(solution)/shard_map/ppermute | solution.py:167
  79.8 7.7 %collective-permute-start.13 = (f32[4,128]{1,0:T(4,128)S(1)}, f32[4,128]{1,0:T(4,128)S(1)}, u32[]{:S(2)}, u32[]{:S(2)}) collective-permute-start(f32[4,128]{1,0:T(4,128)S(1)} %add.419), channel_id=1, source_target_pairs={{0,128},{32,160},{64,192},{96,224},{128,0},{160,32},{192,64},{224,... | collective-permute-start | bytes 6152 | tf_op jit(solution)/shard_map/ppermute | solution.py:167
  93.9 20.3 %collective-permute-start.20 = (f32[16,1,2,64]{0,3,2,1:T(8,128)S(1)}, f32[16,1,2,64]{0,3,2,1:T(8,128)S(1)}, u32[]{:S(2)}, u32[]{:S(2)}) collective-permute-start(f32[16,1,2,64]{0,3,2,1:T(8,128)S(1)} %get-tuple-element.68), channel_id=1, source_target_pairs={{32,0},{64,32},{96,64},{128,96},{160,128},{192,160},{224,192},{33,... | collective-permute-start | bytes 24584 | tf_op jit(solution)/shard_map/ppermute | solution.py:24
  95.2 21.5 %collective-permute-start.21 = (f32[16,1,2,64]{0,3,2,1:T(8,128)S(1)}, f32[16,1,2,64]{0,3,2,1:T(8,128)S(1)}, u32[]{:S(2)}, u32[]{:S(2)}) collective-permute-start(f32[16,1,2,64]{0,3,2,1:T(8,128)S(1)} %get-tuple-element.67), channel_id=1, source_target_pairs={{0,32},{32,64},{64,96},{96,128},{128,160},{160,192},{192,224},{1,3... | collective-permute-start | bytes 24584 | tf_op jit(solution)/shard_map/ppermute | solution.py:23
  100.5 7.2 %collective-permute-start.26 = (f32[16,1,1,32]{0,3,1,2:T(8,128)S(1)}, f32[16,1,1,32]{0,3,1,2:T(8,128)S(1)}, u32[]{:S(2)}, u32[]{:S(2)}) collective-permute-start(f32[16,1,1,32]{0,3,1,2:T(8,128)S(1)} %get-tuple-element.96), channel_id=1, source_target_pairs={{32,0},{64,32},{96,64},{128,96},{160,128},{192,160},{224,192},{33,... | collective-permute-start | bytes 6152 | tf_op jit(solution)/shard_map/ppermute | solution.py:24
  101.8 10.4 %collective-permute-start.27 = (f32[16,1,1,32]{0,3,1,2:T(8,128)S(1)}, f32[16,1,1,32]{0,3,1,2:T(8,128)S(1)}, u32[]{:S(2)}, u32[]{:S(2)}) collective-permute-start(f32[16,1,1,32]{0,3,1,2:T(8,128)S(1)} %get-tuple-element.95), channel_id=1, source_target_pairs={{0,32},{32,64},{64,96},{96,128},{128,160},{160,192},{192,224},{1,3... | collective-permute-start | bytes 6152 | tf_op jit(solution)/shard_map/ppermute | solution.py:23
  106.4 33.5 %collective-permute-start.14 = (f32[16,1,4,128]{3,0,2,1:T(8,128)S(1)}, f32[16,1,4,128]{3,0,2,1:T(8,128)S(1)}, u32[]{:S(2)}, u32[]{:S(2)}) collective-permute-start(f32[16,1,4,128]{3,0,2,1:T(8,128)S(1)} %get-tuple-element.64), channel_id=1, source_target_pairs={{32,0},{64,32},{96,64},{128,96},{160,128},{192,160},{224,192},{33,... | collective-permute-start | bytes 98312 | tf_op jit(solution)/shard_map/ppermute | solution.py:24
  107.7 32.2 %collective-permute-start.15 = (f32[16,1,4,128]{3,0,2,1:T(8,128)S(1)}, f32[16,1,4,128]{3,0,2,1:T(8,128)S(1)}, u32[]{:S(2)}, u32[]{:S(2)}) collective-permute-start(f32[16,1,4,128]{3,0,2,1:T(8,128)S(1)} %get-tuple-element.63), channel_id=1, source_target_pairs={{0,32},{32,64},{64,96},{96,128},{128,160},{160,192},{192,224},{1,3... | collective-permute-start | bytes 98312 | tf_op jit(solution)/shard_map/ppermute | solution.py:23
  114.2 5.6 %collective-permute-start.29 = (f32[16,4,1,32]{0,3,1,2:T(8,128)S(1)}, f32[16,4,1,32]{0,3,1,2:T(8,128)S(1)}, u32[]{:S(2)}, u32[]{:S(2)}) collective-permute-start(f32[16,4,1,32]{0,3,1,2:T(8,128)S(1)} %pad_maximum_fusion.176), channel_id=1, source_target_pairs={{0,4},{4,8},{8,12},{12,16},{16,20},{20,24},{24,28},{1,5},{5,9},{9,... | collective-permute-start | bytes 24584 | tf_op jit(solution)/shard_map/ppermute | solution.py:23
  119.8 6.7 %collective-permute-start.31 = (f32[16,4,3,1]{0,3,1,2:T(1,128)S(1)}, f32[16,4,3,1]{0,3,1,2:T(1,128)S(1)}, u32[]{:S(2)}, u32[]{:S(2)}) collective-permute-start(f32[16,4,3,1]{0,3,1,2:T(1,128)S(1)} %get-tuple-element.76), channel_id=1, source_target_pairs={{0,1},{1,2},{2,3},{4,5},{5,6},{6,7},{8,9},{9,10},{10,11},{12,13},{... | collective-permute-start | bytes 2312 | tf_op jit(solution)/shard_map/ppermute | solution.py:23
  123.3 5.7 %collective-permute-start.30 = (f32[16,4,3,1]{0,3,1,2:T(1,128)S(1)}, f32[16,4,3,1]{0,3,1,2:T(1,128)S(1)}, u32[]{:S(2)}, u32[]{:S(2)}) collective-permute-start(f32[16,4,3,1]{0,3,1,2:T(1,128)S(1)} %get-tuple-element.75), channel_id=1, source_target_pairs={{1,0},{2,1},{3,2},{5,4},{6,5},{7,6},{9,8},{10,9},{11,10},{13,12},{... | collective-permute-start | bytes 2312 | tf_op jit(solution)/shard_map/ppermute | solution.py:24
  126.5 5.4 %collective-permute-start.23 = (f32[16,6,1,64]{3,0,2,1:T(8,128)S(1)}, f32[16,6,1,64]{3,0,2,1:T(8,128)S(1)}, u32[]{:S(2)}, u32[]{:S(2)}) collective-permute-start(f32[16,6,1,64]{3,0,2,1:T(8,128)S(1)} %get-tuple-element.89), channel_id=1, source_target_pairs={{0,4},{4,8},{8,12},{12,16},{16,20},{20,24},{24,28},{1,5},{5,9},{9,... | collective-permute-start | bytes 73736 | tf_op jit(solution)/shard_map/ppermute | solution.py:23
  132.7 12.3 %collective-permute-start.24 = (f32[16,6,4,1]{3,0,2,1:T(8,128)}, f32[16,6,4,1]{3,0,2,1:T(8,128)S(1)}, u32[]{:S(2)}, u32[]{:S(2)}) collective-permute-start(f32[16,6,4,1]{3,0,2,1:T(8,128)} %get-tuple-element.79), channel_id=1, source_target_pairs={{1,0},{2,1},{3,2},{5,4},{6,5},{7,6},{9,8},{10,9},{11,10},{13,12},{... | collective-permute-start | bytes 4616 | tf_op jit(solution)/shard_map/ppermute | solution.py:24
  134.0 11.1 %collective-permute-start.25 = (f32[16,6,4,1]{3,0,2,1:T(8,128)}, f32[16,6,4,1]{3,0,2,1:T(8,128)}, u32[]{:S(2)}, u32[]{:S(2)}) collective-permute-start(f32[16,6,4,1]{3,0,2,1:T(8,128)} %get-tuple-element.80), channel_id=1, source_target_pairs={{0,1},{1,2},{2,3},{4,5},{5,6},{6,7},{8,9},{9,10},{10,11},{12,13},{... | collective-permute-start | bytes 4616 | tf_op jit(solution)/shard_map/ppermute | solution.py:23
  140.7 7.2 %collective-permute-start.16 = (f32[16,10,1,128]{3,0,2,1:T(8,128)}, f32[16,10,1,128]{3,0,2,1:T(8,128)S(1)}, u32[]{:S(2)}, u32[]{:S(2)}) collective-permute-start(f32[16,10,1,128]{3,0,2,1:T(8,128)} %get-tuple-element.50), channel_id=1, source_target_pairs={{4,0},{8,4},{12,8},{16,12},{20,16},{24,20},{28,24},{5,1},{9,5},{13... | collective-permute-start | bytes 245768 | tf_op jit(solution)/shard_map/ppermute | solution.py:24
  142.7 6.0 %collective-permute-start.17 = (f32[16,10,1,128]{3,0,2,1:T(8,128)}, f32[16,10,1,128]{3,0,2,1:T(8,128)S(1)}, u32[]{:S(2)}, u32[]{:S(2)}) collective-permute-start(f32[16,10,1,128]{3,0,2,1:T(8,128)} %get-tuple-element.49), channel_id=1, source_target_pairs={{0,4},{4,8},{8,12},{12,16},{16,20},{20,24},{24,28},{1,5},{5,9},{9,... | collective-permute-start | bytes 245768 | tf_op jit(solution)/shard_map/ppermute | solution.py:23
  150.6 15.0 %collective-permute-start.19 = (f32[16,10,6,1]{3,0,2,1:T(8,128)}, f32[16,10,6,1]{3,0,2,1:T(8,128)}, u32[]{:S(2)}, u32[]{:S(2)}) collective-permute-start(f32[16,10,6,1]{3,0,2,1:T(8,128)} %get-tuple-element.38), channel_id=1, source_target_pairs={{0,1},{1,2},{2,3},{4,5},{5,6},{6,7},{8,9},{9,10},{10,11},{12,13},{... | collective-permute-start | bytes 11528 | tf_op jit(solution)/shard_map/ppermute | solution.py:23
  154.6 15.8 %collective-permute-start.18 = (f32[16,10,6,1]{3,0,2,1:T(8,128)}, f32[16,10,6,1]{3,0,2,1:T(8,128)}, u32[]{:S(2)}, u32[]{:S(2)}) collective-permute-start(f32[16,10,6,1]{3,0,2,1:T(8,128)} %get-tuple-element.37), channel_id=1, source_target_pairs={{1,0},{2,1},{3,2},{5,4},{6,5},{7,6},{9,8},{10,9},{11,10},{13,12},{... | collective-permute-start | bytes 11528 | tf_op jit(solution)/shard_map/ppermute | solution.py:24
  172.1 10.4 %collective-permute-start.32 = (f32[16,1,4,128]{3,0,2,1:T(8,128)S(1)}, f32[16,1,4,128]{3,0,2,1:T(8,128)S(1)}, u32[]{:S(2)}, u32[]{:S(2)}) collective-permute-start(f32[16,1,4,128]{3,0,2,1:T(8,128)S(1)} %get-tuple-element.60), channel_id=1, source_target_pairs={{32,0},{64,32},{96,64},{128,96},{160,128},{192,160},{224,192},{33,... | collective-permute-start | bytes 98312 | tf_op jit(solution)/shard_map/ppermute | solution.py:24
  173.4 9.1 %collective-permute-start.33 = (f32[16,1,4,128]{3,0,2,1:T(8,128)S(1)}, f32[16,1,4,128]{3,0,2,1:T(8,128)S(1)}, u32[]{:S(2)}, u32[]{:S(2)}) collective-permute-start(f32[16,1,4,128]{3,0,2,1:T(8,128)S(1)} %get-tuple-element.59), channel_id=1, source_target_pairs={{0,32},{32,64},{64,96},{96,128},{128,160},{160,192},{192,224},{1,3... | collective-permute-start | bytes 98312 | tf_op jit(solution)/shard_map/ppermute | solution.py:23
  178.8 12.3 %collective-permute-start.43 = (f32[16,10,6,1]{3,0,2,1:T(8,128)S(1)}, f32[16,10,6,1]{3,0,2,1:T(8,128)S(1)}, u32[]{:S(2)}, u32[]{:S(2)}) collective-permute-start(f32[16,10,6,1]{3,0,2,1:T(8,128)S(1)} %get-tuple-element.36), channel_id=1, source_target_pairs={{0,1},{1,2},{2,3},{4,5},{5,6},{6,7},{8,9},{9,10},{10,11},{12,13},{... | collective-permute-start | bytes 11528 | tf_op jit(solution)/shard_map/ppermute | solution.py:23
  181.2 14.1 %collective-permute-start.42 = (f32[16,10,6,1]{3,0,2,1:T(8,128)S(1)}, f32[16,10,6,1]{3,0,2,1:T(8,128)S(1)}, u32[]{:S(2)}, u32[]{:S(2)}) collective-permute-start(f32[16,10,6,1]{3,0,2,1:T(8,128)S(1)} %get-tuple-element.35), channel_id=1, source_target_pairs={{1,0},{2,1},{3,2},{5,4},{6,5},{7,6},{9,8},{10,9},{11,10},{13,12},{... | collective-permute-start | bytes 11528 | tf_op jit(solution)/shard_map/ppermute | solution.py:24
  182.5 13.1 %collective-permute-start.34 = (f32[16,10,1,128]{3,0,2,1:T(8,128)S(1)}, f32[16,10,1,128]{3,0,2,1:T(8,128)S(1)}, u32[]{:S(2)}, u32[]{:S(2)}) collective-permute-start(f32[16,10,1,128]{3,0,2,1:T(8,128)S(1)} %get-tuple-element.46), channel_id=1, source_target_pairs={{4,0},{8,4},{12,8},{16,12},{20,16},{24,20},{28,24},{5,1},{9,5},{13... | collective-permute-start | bytes 245768 | tf_op jit(solution)/shard_map/ppermute | solution.py:24
  184.4 11.2 %collective-permute-start.35 = (f32[16,10,1,128]{3,0,2,1:T(8,128)S(1)}, f32[16,10,1,128]{3,0,2,1:T(8,128)S(1)}, u32[]{:S(2)}, u32[]{:S(2)}) collective-permute-start(f32[16,10,1,128]{3,0,2,1:T(8,128)S(1)} %get-tuple-element.45), channel_id=1, source_target_pairs={{0,4},{4,8},{8,12},{12,16},{16,20},{20,24},{24,28},{1,5},{5,9},{9,... | collective-permute-start | bytes 245768 | tf_op jit(solution)/shard_map/ppermute | solution.py:23
  195.9 11.0 %collective-permute-start.37 = (f32[16,10,6,1]{3,0,2,1:T(8,128)S(1)}, f32[16,10,6,1]{3,0,2,1:T(8,128)S(1)}, u32[]{:S(2)}, u32[]{:S(2)}) collective-permute-start(f32[16,10,6,1]{3,0,2,1:T(8,128)S(1)} %get-tuple-element.34), channel_id=1, source_target_pairs={{0,1},{1,2},{2,3},{4,5},{5,6},{6,7},{8,9},{9,10},{10,11},{12,13},{... | collective-permute-start | bytes 11528 | tf_op jit(solution)/shard_map/ppermute | solution.py:23
  198.1 13.0 %collective-permute-start.36 = (f32[16,10,6,1]{3,0,2,1:T(8,128)S(1)}, f32[16,10,6,1]{3,0,2,1:T(8,128)S(1)}, u32[]{:S(2)}, u32[]{:S(2)}) collective-permute-start(f32[16,10,6,1]{3,0,2,1:T(8,128)S(1)} %get-tuple-element.33), channel_id=1, source_target_pairs={{1,0},{2,1},{3,2},{5,4},{6,5},{7,6},{9,8},{10,9},{11,10},{13,12},{... | collective-permute-start | bytes 11528 | tf_op jit(solution)/shard_map/ppermute | solution.py:24
  226.3 7.1 %collective-permute-start.48 = (f32[36,128]{1,0:T(8,128)S(1)}, f32[36,128]{1,0:T(8,128)S(1)}, u32[]{:S(2)}, u32[]{:S(2)}) collective-permute-start(f32[36,128]{1,0:T(8,128)S(1)} %add.469), channel_id=1, source_target_pairs={{0,64},{32,96},{64,0},{96,32},{128,192},{160,224},{192,128},{224,1... | collective-permute-start | bytes 55304 | tf_op jit(solution)/shard_map/ppermute | solution.py:167
  233.4 5.3 %collective-permute-start.49 = (f32[36,128]{1,0:T(8,128)S(1)}, f32[36,128]{1,0:T(8,128)S(1)}, u32[]{:S(2)}, u32[]{:S(2)}) collective-permute-start(f32[36,128]{1,0:T(8,128)S(1)} %add.470), channel_id=1, source_target_pairs={{0,2},{1,3},{2,0},{3,1},{4,6},{5,7},{6,4},{7,5},{8,10},{9,11},{10,... | collective-permute-start | bytes 55304 | tf_op jit(solution)/shard_map/ppermute | solution.py:167
  238.7 5.3 %collective-permute-start.50 = (f32[36,128]{1,0:T(8,128)S(1)}, f32[36,128]{1,0:T(8,128)S(1)}, u32[]{:S(2)}, u32[]{:S(2)}) collective-permute-start(f32[36,128]{1,0:T(8,128)S(1)} %add.471), channel_id=1, source_target_pairs={{0,16},{4,20},{8,24},{12,28},{16,0},{20,4},{24,8},{28,12},{1,17},{... | collective-permute-start | bytes 55304 | tf_op jit(solution)/shard_map/ppermute | solution.py:167
  244.0 17.7 %collective-permute-start.51 = (f32[36,128]{1,0:T(8,128)S(1)}, f32[36,128]{1,0:T(8,128)S(1)}, u32[]{:S(2)}, u32[]{:S(2)}) collective-permute-start(f32[36,128]{1,0:T(8,128)S(1)} %add.472), channel_id=1, source_target_pairs={{0,128},{32,160},{64,192},{96,224},{128,0},{160,32},{192,64},{224,... | collective-permute-start | bytes 55304 | tf_op jit(solution)/shard_map/ppermute | solution.py:167
  316.9 20.2 %collective-permute-start.58 = (f32[16,1,2,64]{0,3,2,1:T(8,128)S(1)}, f32[16,1,2,64]{0,3,2,1:T(8,128)S(1)}, u32[]{:S(2)}, u32[]{:S(2)}) collective-permute-start(f32[16,1,2,64]{0,3,2,1:T(8,128)S(1)} %get-tuple-element.58), channel_id=1, source_target_pairs={{32,0},{64,32},{96,64},{128,96},{160,128},{192,160},{224,192},{33,... | collective-permute-start | bytes 24584 | tf_op jit(solution)/shard_map/ppermute | solution.py:24
  318.2 21.4 %collective-permute-start.59 = (f32[16,1,2,64]{0,3,2,1:T(8,128)S(1)}, f32[16,1,2,64]{0,3,2,1:T(8,128)S(1)}, u32[]{:S(2)}, u32[]{:S(2)}) collective-permute-start(f32[16,1,2,64]{0,3,2,1:T(8,128)S(1)} %get-tuple-element.57), channel_id=1, source_target_pairs={{0,32},{32,64},{64,96},{96,128},{128,160},{160,192},{192,224},{1,3... | collective-permute-start | bytes 24584 | tf_op jit(solution)/shard_map/ppermute | solution.py:23
  323.5 7.2 %collective-permute-start.64 = (f32[16,1,1,32]{0,3,1,2:T(8,128)S(1)}, f32[16,1,1,32]{0,3,1,2:T(8,128)S(1)}, u32[]{:S(2)}, u32[]{:S(2)}) collective-permute-start(f32[16,1,1,32]{0,3,1,2:T(8,128)S(1)} %get-tuple-element.94), channel_id=1, source_target_pairs={{32,0},{64,32},{96,64},{128,96},{160,128},{192,160},{224,192},{33,... | collective-permute-start | bytes 6152 | tf_op jit(solution)/shard_map/ppermute | solution.py:24
  324.8 10.4 %collective-permute-start.65 = (f32[16,1,1,32]{0,3,1,2:T(8,128)S(1)}, f32[16,1,1,32]{0,3,1,2:T(8,128)S(1)}, u32[]{:S(2)}, u32[]{:S(2)}) collective-permute-start(f32[16,1,1,32]{0,3,1,2:T(8,128)S(1)} %get-tuple-element.93), channel_id=1, source_target_pairs={{0,32},{32,64},{64,96},{96,128},{128,160},{160,192},{192,224},{1,3... | collective-permute-start | bytes 6152 | tf_op jit(solution)/shard_map/ppermute | solution.py:23
  329.3 31.2 %collective-permute-start.52 = (f32[16,1,4,128]{3,0,2,1:T(8,128)S(1)}, f32[16,1,4,128]{3,0,2,1:T(8,128)S(1)}, u32[]{:S(2)}, u32[]{:S(2)}) collective-permute-start(f32[16,1,4,128]{3,0,2,1:T(8,128)S(1)} %get-tuple-element.56), channel_id=1, source_target_pairs={{32,0},{64,32},{96,64},{128,96},{160,128},{192,160},{224,192},{33,... | collective-permute-start | bytes 98312 | tf_op jit(solution)/shard_map/ppermute | solution.py:24
  330.7 29.9 %collective-permute-start.53 = (f32[16,1,4,128]{3,0,2,1:T(8,128)S(1)}, f32[16,1,4,128]{3,0,2,1:T(8,128)S(1)}, u32[]{:S(2)}, u32[]{:S(2)}) collective-permute-start(f32[16,1,4,128]{3,0,2,1:T(8,128)S(1)} %get-tuple-element.55), channel_id=1, source_target_pairs={{0,32},{32,64},{64,96},{96,128},{128,160},{160,192},{192,224},{1,3... | collective-permute-start | bytes 98312 | tf_op jit(solution)/shard_map/ppermute | solution.py:23
  337.2 5.6 %collective-permute-start.67 = (f32[16,4,1,32]{0,3,1,2:T(8,128)S(1)}, f32[16,4,1,32]{0,3,1,2:T(8,128)S(1)}, u32[]{:S(2)}, u32[]{:S(2)}) collective-permute-start(f32[16,4,1,32]{0,3,1,2:T(8,128)S(1)} %pad_maximum_fusion.177), channel_id=1, source_target_pairs={{0,4},{4,8},{8,12},{12,16},{16,20},{20,24},{24,28},{1,5},{5,9},{9,... | collective-permute-start | bytes 24584 | tf_op jit(solution)/shard_map/ppermute | solution.py:23
  342.8 5.4 %collective-permute-start.69 = (f32[16,4,3,1]{0,3,1,2:T(1,128)S(1)}, f32[16,4,3,1]{0,3,1,2:T(1,128)S(1)}, u32[]{:S(2)}, u32[]{:S(2)}) collective-permute-start(f32[16,4,3,1]{0,3,1,2:T(1,128)S(1)} %get-tuple-element.70), channel_id=1, source_target_pairs={{0,1},{1,2},{2,3},{4,5},{5,6},{6,7},{8,9},{9,10},{10,11},{12,13},{... | collective-permute-start | bytes 2312 | tf_op jit(solution)/shard_map/ppermute | solution.py:23
  345.0 5.9 %collective-permute-start.68 = (f32[16,4,3,1]{0,3,1,2:T(1,128)S(1)}, f32[16,4,3,1]{0,3,1,2:T(1,128)S(1)}, u32[]{:S(2)}, u32[]{:S(2)}) collective-permute-start(f32[16,4,3,1]{0,3,1,2:T(1,128)S(1)} %get-tuple-element.69), channel_id=1, source_target_pairs={{1,0},{2,1},{3,2},{5,4},{6,5},{7,6},{9,8},{10,9},{11,10},{13,12},{... | collective-permute-start | bytes 2312 | tf_op jit(solution)/shard_map/ppermute | solution.py:24
  348.2 5.4 %collective-permute-start.61 = (f32[16,6,1,64]{3,0,2,1:T(8,128)S(1)}, f32[16,6,1,64]{3,0,2,1:T(8,128)S(1)}, u32[]{:S(2)}, u32[]{:S(2)}) collective-permute-start(f32[16,6,1,64]{3,0,2,1:T(8,128)S(1)} %get-tuple-element.83), channel_id=1, source_target_pairs={{0,4},{4,8},{8,12},{12,16},{16,20},{20,24},{24,28},{1,5},{5,9},{9,... | collective-permute-start | bytes 73736 | tf_op jit(solution)/shard_map/ppermute | solution.py:23
  353.8 11.3 %collective-permute-start.62 = (f32[16,6,4,1]{3,0,2,1:T(8,128)S(1)}, f32[16,6,4,1]{3,0,2,1:T(8,128)S(1)}, u32[]{:S(2)}, u32[]{:S(2)}) collective-permute-start(f32[16,6,4,1]{3,0,2,1:T(8,128)S(1)} %get-tuple-element.73), channel_id=1, source_target_pairs={{1,0},{2,1},{3,2},{5,4},{6,5},{7,6},{9,8},{10,9},{11,10},{13,12},{... | collective-permute-start | bytes 4616 | tf_op jit(solution)/shard_map/ppermute | solution.py:24
  355.1 10.0 %collective-permute-start.63 = (f32[16,6,4,1]{3,0,2,1:T(8,128)S(1)}, f32[16,6,4,1]{3,0,2,1:T(8,128)S(1)}, u32[]{:S(2)}, u32[]{:S(2)}) collective-permute-start(f32[16,6,4,1]{3,0,2,1:T(8,128)S(1)} %get-tuple-element.74), channel_id=1, source_target_pairs={{0,1},{1,2},{2,3},{4,5},{5,6},{6,7},{8,9},{9,10},{10,11},{12,13},{... | collective-permute-start | bytes 4616 | tf_op jit(solution)/shard_map/ppermute | solution.py:23
  362.7 5.8 %collective-permute-start.55 = (f32[16,10,1,128]{3,0,2,1:T(8,128)S(1)}, f32[16,10,1,128]{3,0,2,1:T(8,128)S(1)}, u32[]{:S(2)}, u32[]{:S(2)}) collective-permute-start(f32[16,10,1,128]{3,0,2,1:T(8,128)S(1)} %get-tuple-element.43), channel_id=1, source_target_pairs={{0,4},{4,8},{8,12},{12,16},{16,20},{20,24},{24,28},{1,5},{5,9},{9,... | collective-permute-start | bytes 245768 | tf_op jit(solution)/shard_map/ppermute | solution.py:23
  369.6 13.0 %collective-permute-start.57 = (f32[16,10,6,1]{3,0,2,1:T(8,128)}, f32[16,10,6,1]{3,0,2,1:T(8,128)}, u32[]{:S(2)}, u32[]{:S(2)}) collective-permute-start(f32[16,10,6,1]{3,0,2,1:T(8,128)} %get-tuple-element.32), channel_id=1, source_target_pairs={{0,1},{1,2},{2,3},{4,5},{5,6},{6,7},{8,9},{9,10},{10,11},{12,13},{... | collective-permute-start | bytes 11528 | tf_op jit(solution)/shard_map/ppermute | solution.py:23
  374.3 13.2 %collective-permute-start.56 = (f32[16,10,6,1]{3,0,2,1:T(8,128)}, f32[16,10,6,1]{3,0,2,1:T(8,128)}, u32[]{:S(2)}, u32[]{:S(2)}) collective-permute-start(f32[16,10,6,1]{3,0,2,1:T(8,128)} %get-tuple-element.31), channel_id=1, source_target_pairs={{1,0},{2,1},{3,2},{5,4},{6,5},{7,6},{9,8},{10,9},{11,10},{13,12},{... | collective-permute-start | bytes 11528 | tf_op jit(solution)/shard_map/ppermute | solution.py:24
  389.0 6.5 %collective-permute-start.70 = (f32[16,1,4,128]{3,0,2,1:T(8,128)S(1)}, f32[16,1,4,128]{3,0,2,1:T(8,128)S(1)}, u32[]{:S(2)}, u32[]{:S(2)}) collective-permute-start(f32[16,1,4,128]{3,0,2,1:T(8,128)S(1)} %get-tuple-element.54), channel_id=1, source_target_pairs={{32,0},{64,32},{96,64},{128,96},{160,128},{192,160},{224,192},{33,... | collective-permute-start | bytes 98312 | tf_op jit(solution)/shard_map/ppermute | solution.py:24
  390.3 6.1 %collective-permute-start.71 = (f32[16,1,4,128]{3,0,2,1:T(8,128)S(1)}, f32[16,1,4,128]{3,0,2,1:T(8,128)S(1)}, u32[]{:S(2)}, u32[]{:S(2)}) collective-permute-start(f32[16,1,4,128]{3,0,2,1:T(8,128)S(1)} %get-tuple-element.53), channel_id=1, source_target_pairs={{0,32},{32,64},{64,96},{96,128},{128,160},{160,192},{192,224},{1,3... | collective-permute-start | bytes 98312 | tf_op jit(solution)/shard_map/ppermute | solution.py:23
  396.5 6.1 %collective-permute-start.72 = (f32[16,10,1,128]{3,0,2,1:T(8,128)S(1)}, f32[16,10,1,128]{3,0,2,1:T(8,128)S(1)}, u32[]{:S(2)}, u32[]{:S(2)}) collective-permute-start(f32[16,10,1,128]{3,0,2,1:T(8,128)S(1)} %get-tuple-element.42), channel_id=1, source_target_pairs={{4,0},{8,4},{12,8},{16,12},{20,16},{24,20},{28,24},{5,1},{9,5},{13... | collective-permute-start | bytes 245768 | tf_op jit(solution)/shard_map/ppermute | solution.py:24
  398.4 5.8 %collective-permute-start.73 = (f32[16,10,1,128]{3,0,2,1:T(8,128)S(1)}, f32[16,10,1,128]{3,0,2,1:T(8,128)S(1)}, u32[]{:S(2)}, u32[]{:S(2)}) collective-permute-start(f32[16,10,1,128]{3,0,2,1:T(8,128)S(1)} %get-tuple-element.41), channel_id=1, source_target_pairs={{0,4},{4,8},{8,12},{12,16},{16,20},{20,24},{24,28},{1,5},{5,9},{9,... | collective-permute-start | bytes 245768 | tf_op jit(solution)/shard_map/ppermute | solution.py:23
  404.4 12.2 %collective-permute-start.75 = (f32[16,10,6,1]{3,0,2,1:T(8,128)S(1)}, f32[16,10,6,1]{3,0,2,1:T(8,128)S(1)}, u32[]{:S(2)}, u32[]{:S(2)}) collective-permute-start(f32[16,10,6,1]{3,0,2,1:T(8,128)S(1)} %get-tuple-element.30), channel_id=1, source_target_pairs={{0,1},{1,2},{2,3},{4,5},{5,6},{6,7},{8,9},{9,10},{10,11},{12,13},{... | collective-permute-start | bytes 11528 | tf_op jit(solution)/shard_map/ppermute | solution.py:23
  407.6 13.2 %collective-permute-start.74 = (f32[16,10,6,1]{3,0,2,1:T(8,128)S(1)}, f32[16,10,6,1]{3,0,2,1:T(8,128)S(1)}, u32[]{:S(2)}, u32[]{:S(2)}) collective-permute-start(f32[16,10,6,1]{3,0,2,1:T(8,128)S(1)} %get-tuple-element.29), channel_id=1, source_target_pairs={{1,0},{2,1},{3,2},{5,4},{6,5},{7,6},{9,8},{10,9},{11,10},{13,12},{... | collective-permute-start | bytes 11528 | tf_op jit(solution)/shard_map/ppermute | solution.py:24
  435.2 7.6 %collective-permute-start.80 = (f32[36,128]{1,0:T(8,128)S(1)}, f32[36,128]{1,0:T(8,128)S(1)}, u32[]{:S(2)}, u32[]{:S(2)}) collective-permute-start(f32[36,128]{1,0:T(8,128)S(1)} %add.504), channel_id=1, source_target_pairs={{0,64},{32,96},{64,0},{96,32},{128,192},{160,224},{192,128},{224,1... | collective-permute-start | bytes 55304 | tf_op jit(solution)/shard_map/ppermute | solution.py:167
  442.9 5.3 %collective-permute-start.81 = (f32[36,128]{1,0:T(8,128)S(1)}, f32[36,128]{1,0:T(8,128)S(1)}, u32[]{:S(2)}, u32[]{:S(2)}) collective-permute-start(f32[36,128]{1,0:T(8,128)S(1)} %add.505), channel_id=1, source_target_pairs={{0,2},{1,3},{2,0},{3,1},{4,6},{5,7},{6,4},{7,5},{8,10},{9,11},{10,... | collective-permute-start | bytes 55304 | tf_op jit(solution)/shard_map/ppermute | solution.py:167
  448.1 5.3 %collective-permute-start.82 = (f32[36,128]{1,0:T(8,128)S(1)}, f32[36,128]{1,0:T(8,128)S(1)}, u32[]{:S(2)}, u32[]{:S(2)}) collective-permute-start(f32[36,128]{1,0:T(8,128)S(1)} %add.506), channel_id=1, source_target_pairs={{0,16},{4,20},{8,24},{12,28},{16,0},{20,4},{24,8},{28,12},{1,17},{... | collective-permute-start | bytes 55304 | tf_op jit(solution)/shard_map/ppermute | solution.py:167
  453.4 9.3 %collective-permute-start.83 = (f32[36,128]{1,0:T(8,128)S(1)}, f32[36,128]{1,0:T(8,128)S(1)}, u32[]{:S(2)}, u32[]{:S(2)}) collective-permute-start(f32[36,128]{1,0:T(8,128)S(1)} %add.507), channel_id=1, source_target_pairs={{0,128},{32,160},{64,192},{96,224},{128,0},{160,32},{192,64},{224,... | collective-permute-start | bytes 55304 | tf_op jit(solution)/shard_map/ppermute | solution.py:167
  (77 other events, 1360.4 us)
